TPU v7x, 32 devices: a whole 2x2x4 slice. The times are simulated.
32 devices in a mesh: samp: 4 (over y, x), box: 8 (over z, core).
Axes of the slice: x: 2, y: 2, z: 4, core: 2. Of those that a mesh axis runs over, the one named last changes fastest.
Arguments:
- pattern_a: float32 [1024, 2, 18432], P('box', None, 'samp'), may hold values from -6 to 6
- children_b: int32 [256, 8], P('box'), may hold values from -1 to 1023, as said below
- children_c: int32 [64, 8], P('box'), may hold values from -1 to 255, as said below
- theta_ab: float32 [96, 128], replicated, may hold values from -0.625 to 0.625
- theta_bc: float32 [128, 160], replicated, may hold values from -0.5 to 0.5
- phi_start_b: int32 [256], P('samp'), may hold values from 0 to 191, as said below
- phi_weight_b: float32 [4, 256], P(None, 'samp'), may hold values from -0.25 to 1
- phi_start_c: int32 [320], P('samp'), may hold values from 0 to 255, as said below
- phi_weight_c: float32 [4, 320], P(None, 'samp'), may hold values from -0.25 to 1
- translation: float32 [316, 2, 51200], P(None, None, 'samp'), may hold values from -0.1875 to 0.1875
- list_src: int32 [64, 32], P('box'), may hold values from 0 to 63
- list_vec: int32 [64, 32], P('box'), may hold values from 0 to 315
Outputs:
- incoming: float32 [64, 2, 51200], P('box', None, 'samp')
Inputs may be any that keep to these rules, and one draw needn't show every extreme that they name: `children_b`: entry o of a row is -1 or the level-A box in octant o = 4 ox + 2 oy + oz of that level-B box; level-B box p and its children lie on the same index of box, boxes p // 32 and c // 128 being equal; every level-A box is the child of exactly one level-B box. `children_c`: entry o of a row is -1 or the level-B box in octant o of that level-C box; p // 8 equals c // 32; every level-B box is the child of exactly one level-C box. phi_start_b[m] is (m * 192 // 256 - 1) or (m * 192 // 256 - 2), modulo 192. phi_start_c[m] is (m * 256 // 320 - 1) or (m * 256 // 320 - 2), modulo 256.
All inputs are finite; a program needn't handle non-finite values.
Results may differ from a plain program's by a relative error of at most 0.000071.
Values sent between devices are 32-bit elements; how exact they have to be, the bound alone decides.
A program may use at most 192 MiB of HBM per device.

v0:
```python
import jax
import jax.numpy as jnp
from jax import lax
from jax.sharding import PartitionSpec as P

SIZE_B = 8
SIZE_C = 16


PRECISE = lax.Precision.HIGHEST


def with_halo(cells, sides, width):
    for axis, dim in sides:
        count = lax.axis_size(axis)
        head = lax.slice_in_dim(cells, 0, width, axis=dim)
        tail = lax.slice_in_dim(cells, cells.shape[dim] - width, cells.shape[dim], axis=dim)
        cells = jnp.concatenate(
            [
                lax.ppermute(tail, axis, [(i, (i + 1) % count) for i in range(count)]),
                cells,
                lax.ppermute(head, axis, [((i + 1) % count, i) for i in range(count)]),
            ],
            axis=dim,
        )
    return cells


def directions(n_theta, n_phi, phi_first, phi_count):
    polar = jnp.pi * (jnp.arange(n_theta, dtype=jnp.int32).astype(jnp.float32) + 0.5) / n_theta
    azimuth = (
        2.0
        * jnp.pi
        * (phi_first + jnp.arange(phi_count, dtype=jnp.int32)).astype(jnp.float32)
        / n_phi
    )
    polar_sine = jnp.sin(polar)[None, :]
    dir_x = jnp.cos(azimuth)[:, None] * polar_sine
    dir_y = jnp.sin(azimuth)[:, None] * polar_sine
    dir_z = jnp.broadcast_to(jnp.cos(polar)[None, :], dir_x.shape)
    return (dir_x, dir_y, dir_z)


def aggregate(level, children, first_box, box_size, n_phi, phi_first):
    box_count = level.shape[0]
    flat = level.reshape(box_count, 2, level.shape[2] * level.shape[3])
    dir_x, dir_y, dir_z = directions(level.shape[3], n_phi, phi_first, level.shape[2])
    summed = jnp.zeros((children.shape[0], 2, flat.shape[2]), jnp.float32)
    for octant in range(8):
        sign_x = 2.0 * (octant >> 2 & 1) - 1.0
        sign_y = 2.0 * (octant >> 1 & 1) - 1.0
        sign_z = 2.0 * (octant & 1) - 1.0
        phase = 0.5 * jnp.pi * box_size * (sign_x * dir_x + sign_y * dir_y + sign_z * dir_z)
        cosine = jnp.cos(phase).reshape(-1)
        sine_part = jnp.sin(phase).reshape(-1)
        child_ids = children[:, octant] - first_box
        present = (children[:, octant] >= 0).astype(jnp.float32)[:, None]
        picked = jnp.take(flat, jnp.clip(child_ids, 0, box_count - 1), axis=0)
        real_part = picked[:, 0] * cosine - picked[:, 1] * sine_part
        imag_part = picked[:, 0] * sine_part + picked[:, 1] * cosine
        summed = summed + jnp.stack([present * real_part, present * imag_part], axis=1)
    return summed


def translate(rows, operators, vectors):
    picked = jnp.take(operators, vectors.reshape(-1), axis=0).reshape(rows.shape)
    real_part = jnp.sum(picked[:, :, 0] * rows[:, :, 0] - picked[:, :, 1] * rows[:, :, 1], axis=1)
    imag_part = jnp.sum(picked[:, :, 0] * rows[:, :, 1] + picked[:, :, 1] * rows[:, :, 0], axis=1)
    return jnp.stack([real_part, imag_part], axis=1)


def interpolate(widened, theta_matrix, phi_start, phi_weight, first_child, n_phi_child):
    grid = jnp.einsum("bcpt,tu->bcpu", widened, theta_matrix, precision=PRECISE)
    local_start = (phi_start - first_child + 2) % n_phi_child
    summed = jnp.zeros((grid.shape[0], 2, phi_start.shape[0], grid.shape[3]), jnp.float32)
    for offset in range(4):
        summed = summed + phi_weight[offset][None, None, :, None] * jnp.take(
            grid, local_start + offset, axis=2
        )
    return summed


def per_device(
    pattern_a,
    children_b,
    children_c,
    theta_ab,
    theta_bc,
    phi_start_b,
    phi_weight_b,
    phi_start_c,
    phi_weight_c,
    translation,
    list_src,
    list_vec,
):
    cycle_size = lax.axis_size("samp")
    samp_place = lax.axis_index("samp")
    box_place = lax.axis_index("box")
    count_a = pattern_a.shape[0]
    count_b = children_b.shape[0]
    count_c = children_c.shape[0]
    theta_a = theta_ab.shape[0]
    theta_b = theta_ab.shape[1]
    phi_a_dev = pattern_a.shape[2] // theta_a
    phi_b_dev = phi_start_b.shape[0]
    phi_c_dev = phi_start_c.shape[0]
    grid_a = pattern_a.reshape(count_a, 2, phi_a_dev, theta_a)
    widened_a = with_halo(grid_a, (("samp", 2),), 2)
    level_b = interpolate(
        widened_a,
        theta_ab,
        phi_start_b,
        phi_weight_b,
        samp_place * phi_a_dev,
        cycle_size * phi_a_dev,
    )
    pattern_b = aggregate(
        level_b,
        children_b,
        box_place * count_a,
        SIZE_B,
        cycle_size * phi_b_dev,
        samp_place * phi_b_dev,
    )
    grid_b = pattern_b.reshape(count_b, 2, phi_b_dev, theta_b)
    widened_b = with_halo(grid_b, (("samp", 2),), 2)
    level_c = interpolate(
        widened_b,
        theta_bc,
        phi_start_c,
        phi_weight_c,
        samp_place * phi_b_dev,
        cycle_size * phi_b_dev,
    )
    pattern_c = aggregate(
        level_c,
        children_c,
        box_place * count_b,
        SIZE_C,
        cycle_size * phi_c_dev,
        samp_place * phi_c_dev,
    )
    samples = pattern_c.shape[2]
    list_len = list_src.shape[1]
    flat_src = list_src.reshape(-1)
    portion = lax.all_gather(pattern_c, "box", axis=0, tiled=True)
    length = portion.shape[0]
    inside = ((flat_src >= 0) & (flat_src < length)).astype(jnp.float32)[:, None, None]
    picked = jnp.take(portion, jnp.clip(flat_src, 0, length - 1), axis=0)
    gathered = inside * picked
    incoming = translate(gathered.reshape(count_c, list_len, 2, samples), translation, list_vec)
    return incoming


def solution(mesh):
    placed = (
        P("box", None, "samp"),
        P("box", None),
        P("box", None),
        P(),
        P(),
        P("samp"),
        P(None, "samp"),
        P("samp"),
        P(None, "samp"),
        P(None, None, "samp"),
        P("box", None),
        P("box", None),
    )
    return jax.shard_map(
        per_device, mesh=mesh, in_specs=placed, out_specs=P("box", None, "samp"), check_vma=False
    )
```

profile of v0, /device:TPU:0, one launch (start us, length us, event | category | flops | bytes accessed | tf_op | source)
XLA Modules:
  0.0 515.8 jit_solution(1576749490784674727)
XLA Ops:
  6.6 8.2 %copy.94 = f32[128,2,4608]{0,2,1:T(8,128)} copy(f32[128,2,4608]{2,1,0:T(2,128)} %param.20) | data formatting | bytes 9437184 | tf_op args[0]
  15.8 3.0 collective-permute-start
  39.2 14.3 %fusion.6 = f32[128,2,52,128]{3,0,2,1:T(8,128)} fusion(f32[128,2,2,96]{0,3,2,1:T(8,128)S(1)} %collective-permute-done.1, f32[128,2,48,96]{0,3,2,1:T(8,128)} %bitcast.434, f32[128,2,2,96]{0,3,2,1:T(8,128)S(1)} %collective-permute-done, f32[96,128]{1,0:T(8,128)S(1)} %copy-done.32), kind=kOutput, calls=%fused_computation.44 | convolution fusion | flops 1965490176 | bytes 11976704 | tf_op jit(solution)/shard_map/bcpt,tu->bcpu/dot_general | solution.py:73
  53.6 7.3 %gather_fusion.5 = f32[64,128,2,128]{3,1,2,0:T(8,128)} fusion(f32[128,2,52,128]{3,0,2,1:T(8,128)} %fusion.6, s32[1024]{0:T(1024)S(1)} %get-tuple-element.186), kind=kCustom, calls=%fused_computation.6.clone | custom fusion | bytes 16777472 | tf_op jit(solution)/shard_map/jit(_take)/gather | solution.py:77
  60.8 7.3 %gather_fusion.4 = f32[64,128,2,128]{3,1,2,0:T(8,128)} fusion(f32[128,2,52,128]{3,0,2,1:T(8,128)} %fusion.6, s32[1024]{0:T(1024)S(1)} %get-tuple-element.187), kind=kCustom, calls=%fused_computation.5.clone | custom fusion | bytes 16777472 | tf_op jit(solution)/shard_map/jit(_take)/gather | solution.py:77
  68.2 7.3 %gather_fusion.3 = f32[64,128,2,128]{3,1,2,0:T(8,128)} fusion(f32[128,2,52,128]{3,0,2,1:T(8,128)} %fusion.6, s32[1024]{0:T(1024)S(1)} %pad_clamp_fusion.23), kind=kCustom, calls=%fused_computation.4.clone | custom fusion | bytes 16777472 | tf_op jit(solution)/shard_map/jit(_take)/gather | solution.py:77
  75.5 7.3 %gather_fusion.2 = f32[64,128,2,128]{3,1,2,0:T(8,128)} fusion(f32[128,2,52,128]{3,0,2,1:T(8,128)} %fusion.6, s32[1024]{0:T(1024)S(1)} %pad_clamp_fusion.24), kind=kCustom, calls=%fused_computation.clone | custom fusion | bytes 16777472 | tf_op jit(solution)/shard_map/jit(_take)/gather | solution.py:77
  82.8 27.9 %fusion = f32[128,2,64,128]{3,0,1,2:T(8,128)} fusion(f32[64,128,2,128]{3,1,2,0:T(8,128)} %gather_fusion.5, f32[64,128,2,128]{3,1,2,0:T(8,128)} %gather_fusion.4, f32[64,128,2,128]{3,1,2,0:T(8,128)} %gather_fusion.3, f32[64,128,2,128]{3,1,2,0:T(8,128)} %gather_fusion.2, f32[64]{0:T(128)S(1)} %get-tuple-element.166, f32[64]{0:T(128)S(1)} %get-tuple-element.167, ...), kind=kLoop, calls=%fused_computation.31 | loop fusion | flops 23068672 | bytes 41944320 | tf_op jit(solution)/shard_map/add | solution.py:77
  110.7 8.9 %copy.95 = f32[128,2,64,128]{0,3,2,1:T(8,128)} copy(f32[128,2,64,128]{3,0,1,2:T(8,128)} %fusion) | data formatting | bytes 16777216 | tf_op jit(solution)/shard_map/add | solution.py:77
  119.6 13.3 %copy.96 = f32[128,2,8192]{2,1,0:T(2,128)} copy(f32[128,2,8192]{0,2,1:T(8,128)} %bitcast.432) | data formatting | bytes 16777216 | tf_op jit(solution)/shard_map/reshape | solution.py:46
  132.9 6.2 %gather_fusion.13 = f32[32,2,8192]{2,1,0:T(2,128)S(1)} fusion(f32[128,2,8192]{2,1,0:T(2,128)} %copy.96, s32[1024]{0:T(1024)S(1)} %get-tuple-element.188), kind=kCustom, calls=%fused_computation.13.clone | custom fusion | bytes 4194432 | tf_op jit(solution)/shard_map/jit(_take)/gather | solution.py:58
  142.1 6.3 %gather_fusion.12 = f32[32,2,8192]{2,1,0:T(2,128)S(1)} fusion(f32[128,2,8192]{2,1,0:T(2,128)} %copy.96, s32[1024]{0:T(1024)} %get-tuple-element.189), kind=kCustom, calls=%fused_computation.12.clone | custom fusion | bytes 4194432 | tf_op jit(solution)/shard_map/jit(_take)/gather | solution.py:58
  153.9 6.3 %gather_fusion.11 = f32[32,2,8192]{2,1,0:T(2,128)S(1)} fusion(f32[128,2,8192]{2,1,0:T(2,128)} %copy.96, s32[1024]{0:T(1024)} %get-tuple-element.190), kind=kCustom, calls=%fused_computation.11.clone | custom fusion | bytes 4194432 | tf_op jit(solution)/shard_map/jit(_take)/gather | solution.py:58
  166.0 6.3 %gather_fusion.10 = f32[32,2,8192]{2,1,0:T(2,128)S(1)} fusion(f32[128,2,8192]{2,1,0:T(2,128)} %copy.96, s32[1024]{0:T(1024)} %get-tuple-element.191), kind=kCustom, calls=%fused_computation.10.clone | custom fusion | bytes 4194432 | tf_op jit(solution)/shard_map/jit(_take)/gather | solution.py:58
  177.8 6.3 %gather_fusion.9 = f32[32,2,8192]{2,1,0:T(2,128)S(1)} fusion(f32[128,2,8192]{2,1,0:T(2,128)} %copy.96, s32[1024]{0:T(1024)} %get-tuple-element.192), kind=kCustom, calls=%fused_computation.9.clone | custom fusion | bytes 4194432 | tf_op jit(solution)/shard_map/jit(_take)/gather | solution.py:58
  189.6 6.5 %gather_fusion.8 = f32[32,2,8192]{2,1,0:T(2,128)S(1)} fusion(f32[128,2,8192]{2,1,0:T(2,128)} %copy.96, s32[1024]{0:T(1024)} %get-tuple-element.193), kind=kCustom, calls=%fused_computation.8.clone | custom fusion | bytes 4194432 | tf_op jit(solution)/shard_map/jit(_take)/gather | solution.py:58
  201.5 7.5 %gather_fusion.7 = f32[32,2,8192]{2,1,0:T(2,128)} fusion(f32[128,2,8192]{2,1,0:T(2,128)} %copy.96, s32[1024]{0:T(1024)} %get-tuple-element.194), kind=kCustom, calls=%fused_computation.7.clone | custom fusion | bytes 4194432 | tf_op jit(solution)/shard_map/jit(_take)/gather | solution.py:58
  208.9 6.3 %gather_fusion.6 = f32[32,2,8192]{2,1,0:T(2,128)S(1)} fusion(f32[128,2,8192]{2,1,0:T(2,128)} %copy.96, s32[1024]{0:T(1024)} %get-tuple-element.195), kind=kCustom, calls=%fused_computation.1.clone | custom fusion | bytes 4194432 | tf_op jit(solution)/shard_map/jit(_take)/gather | solution.py:58
  232.6 3.8 fusion.12
  236.5 4.7 copy.128
  241.2 5.6 %gather_fusion.17 = f32[80,32,2,160]{3,1,2,0:T(8,128)} fusion(f32[32,2,68,160]{3,0,2,1:T(8,128)} %copy.128, s32[1024]{0:T(1024)} %get-tuple-element.200), kind=kCustom, calls=%fused_computation.16.clone | custom fusion | bytes 6553920 | tf_op jit(solution)/shard_map/jit(_take)/gather | solution.py:77
  246.8 5.7 %gather_fusion.16 = f32[80,32,2,160]{3,1,2,0:T(8,128)} fusion(f32[32,2,68,160]{3,0,2,1:T(8,128)} %copy.128, s32[1024]{0:T(1024)} %get-tuple-element.201), kind=kCustom, calls=%fused_computation.15.clone | custom fusion | bytes 6553920 | tf_op jit(solution)/shard_map/jit(_take)/gather | solution.py:77
  252.4 5.4 %gather_fusion.15 = f32[80,32,2,160]{3,1,2,0:T(8,128)} fusion(f32[32,2,68,160]{3,0,2,1:T(8,128)} %copy.128, s32[1024]{0:T(1024)S(1)} %pad_clamp_fusion.11), kind=kCustom, calls=%fused_computation.14.clone | custom fusion | bytes 6553920 | tf_op jit(solution)/shard_map/jit(_take)/gather | solution.py:77
  257.9 5.6 %gather_fusion.14 = f32[80,32,2,160]{3,1,2,0:T(8,128)} fusion(f32[32,2,68,160]{3,0,2,1:T(8,128)} %copy.128, s32[1024]{0:T(1024)} %pad_clamp_fusion.12), kind=kCustom, calls=%fused_computation.2.clone | custom fusion | bytes 6553920 | tf_op jit(solution)/shard_map/jit(_take)/gather | solution.py:77
  263.5 8.4 %fusion.3 = f32[32,2,80,160]{3,0,1,2:T(8,128)S(1)} fusion(f32[80,32,2,160]{3,1,2,0:T(8,128)} %gather_fusion.17, f32[80,32,2,160]{3,1,2,0:T(8,128)} %gather_fusion.16, f32[80,32,2,160]{3,1,2,0:T(8,128)} %gather_fusion.15, f32[80,32,2,160]{3,1,2,0:T(8,128)} %gather_fusion.14, f32[80]{0:T(128)S(1)} %copy-done.62, f32[80]{0:T(128)S(1)} %copy-done.63, ...), kind=kLoop, calls=%fused_computation.38 | loop fusion | flops 9011200 | bytes 16385600 | tf_op jit(solution)/shard_map/add | solution.py:77
  272.0 5.4 %copy.153 = f32[32,2,80,160]{3,2,1,0:T(8,128)} copy(f32[32,2,80,160]{3,0,1,2:T(8,128)S(1)} %fusion.3) | data formatting | bytes 6553600 | tf_op jit(solution)/shard_map/reshape | solution.py:46
  277.4 6.4 %reshape.2065 = f32[32,2,12800]{2,1,0:T(2,128)S(1)} reshape(f32[32,2,80,160]{3,2,1,0:T(8,128)} %copy.153) | data formatting | bytes 6553600 | tf_op jit(solution)/shard_map/reshape | solution.py:46
  313.0 55.5 %gather_fusion = f32[256,2,12800]{2,1,0:T(2,128)} fusion(f32[316,2,12800]{2,1,0:T(2,128)} %param.29, s32[1024]{0:T(1024)S(1)} %pad_clamp_fusion.25), kind=kCustom, calls=%fused_computation.24 | custom fusion | bytes 52429824 | tf_op jit(solution)/shard_map/jit(_take)/gather | solution.py:66
  368.6 18.6 %broadcast_select_fusion = f32[8,32,2,12800]{3,2,1,0:T(2,128)} fusion(f32[8,32,2,12800]{3,2,1,0:T(2,128)} %bitcast.431, pred[8,32]{1,0:T(8,128)(4,1)S(1)} %compare_and_fusion.1), kind=kLoop, calls=%fused_computation.27 | loop fusion | flops 6553600 | bytes 52429056 | tf_op jit(solution)/shard_map/jit(_take)/select_n | solution.py:66
  387.2 45.8 %gather_fusion.1 = f32[256,2,12800]{2,1,0:T(2,128)} fusion(f32[64,2,12800]{2,1,0:T(2,128)} %all-gather.2.cloned.1.call-done, s32[1024]{0:T(1024)S(1)} %pad_clamp_fusion), kind=kCustom, calls=%fused_computation.25 | custom fusion | bytes 52429824 | tf_op jit(solution)/shard_map/jit(_take)/gather | solution.py:150
  433.0 19.8 %select_multiply_fusion = f32[8,32,2,12800]{3,2,1,0:T(2,128)} fusion(f32[8,32,2,12800]{3,2,1,0:T(2,128)} %bitcast.430, pred[8,32]{1,0:T(8,128)(4,1)S(1)} %get-tuple-element.121, f32[8,32]{1,0:T(8,128)S(1)} %get-tuple-element.120), kind=kLoop, calls=%fused_computation.26 | loop fusion | flops 13107200 | bytes 52430080 | tf_op jit(solution)/shard_map/mul | solution.py:151
  452.8 54.2 %subtract_reduce_fusion = (f32[8,12800]{1,0:T(8,128)S(1)}, f32[8,12800]{1,0:T(8,128)S(1)}) fusion(f32[8,32,2,12800]{3,2,1,0:T(2,128)} %select_multiply_fusion, f32[8,32,2,12800]{3,2,1,0:T(2,128)} %broadcast_select_fusion), kind=kLoop, calls=%fused_computation.29 | loop fusion | flops 26009600 | bytes 53248000 | tf_op jit(solution)/shard_map/reduce_sum | solution.py:67
  (275 shorter events, 99.4 us)
Async XLA Ops:
  6.5 226.1 %copy-start = (f32[128,160]{0,1:T(8,128)S(1)}, f32[128,160]{0,1:T(8,128)}, u32[]{:S(2)}) copy-start(f32[128,160]{0,1:T(8,128)} %param.24) | copy-start | bytes 245764
  6.5 13.6 %copy-start.67 = (s32[80]{0:T(128)S(1)}, s32[80]{0:T(128)}, u32[]{:S(2)}) copy-start(s32[80]{0:T(128)} %param.27) | copy-start | bytes 964
  6.5 14.8 %copy-start.68 = (s32[64]{0:T(128)S(1)}, s32[64]{0:T(128)}, u32[]{:S(2)}) copy-start(s32[64]{0:T(128)} %param.25) | copy-start | bytes 772
  6.5 14.9 %copy-start.18 = (s32[8,8]{1,0:T(8,128)S(1)}, s32[8,8]{1,0:T(8,128)}, u32[]{:S(2)}) copy-start(s32[8,8]{1,0:T(8,128)} %param.22) | copy-start | bytes 772
  6.5 17.8 %copy-start.65 = (f32[4,64]{1,0:T(4,128)S(1)}, f32[4,64]{1,0:T(4,128)}, u32[]{:S(2)}) copy-start(f32[4,64]{1,0:T(4,128)} %param.26) | copy-start | bytes 3076
  6.5 17.8 %copy-start.66 = (f32[4,80]{1,0:T(4,128)S(1)}, f32[4,80]{1,0:T(4,128)}, u32[]{:S(2)}) copy-start(f32[4,80]{1,0:T(4,128)} %param.28) | copy-start | bytes 3844
  6.6 23.1 %copy-start.33 = (s32[32,8]{0,1:T(8,128)S(1)}, s32[32,8]{0,1:T(8,128)}, u32[]{:S(2)}) copy-start(s32[32,8]{0,1:T(8,128)} %param.21) | copy-start | bytes 3076
  6.6 32.7 %copy-start.32 = (f32[96,128]{1,0:T(8,128)S(1)}, f32[96,128]{1,0:T(8,128)}, u32[]{:S(2)}) copy-start(f32[96,128]{1,0:T(8,128)} %param.23) | copy-start | bytes 147460
  6.6 380.6 %all-gather.2.cloned.1.call-start = ((), (), s32[]{:S(2)}) async-start(), calls=%async_computation | async-start | bytes 7372800 | tf_op jit(solution)/shard_map/all_gather | solution.py:147
  15.8 23.4 %collective-permute-start = (f32[128,2,2,96]{0,3,2,1:T(8,128)S(1)}, f32[128,2,2,96]{0,3,2,1:T(8,128)S(1)}, u32[]{:S(2)}, u32[]{:S(2)}) collective-permute-start(f32[128,2,2,96]{0,3,2,1:T(8,128)S(1)} %get-tuple-element.61), channel_id=1, source_target_pairs={{0,8},{8,16},{16,24},{24,0},{1,9},{9,17},{17,25},{25,1},{2,10},{10... | collective-permute-start | bytes 589832 | tf_op jit(solution)/shard_map/ppermute | solution.py:20
  18.9 20.4 %collective-permute-start.1 = (f32[128,2,2,96]{0,3,2,1:T(8,128)S(1)}, f32[128,2,2,96]{0,3,2,1:T(8,128)S(1)}, u32[]{:S(2)}, u32[]{:S(2)}) collective-permute-start(f32[128,2,2,96]{0,3,2,1:T(8,128)S(1)} %get-tuple-element.62), channel_id=1, source_target_pairs={{8,0},{16,8},{24,16},{0,24},{9,1},{17,9},{25,17},{1,25},{10,2},{18... | collective-permute-start | bytes 589832 | tf_op jit(solution)/shard_map/ppermute | solution.py:22
  201.5 13.8 %copy-start.50 = (pred[32]{0:T(512)(128)(4,1)S(1)}, pred[32]{0:T(512)(128)(4,1)}, u32[]{:S(2)}) copy-start(pred[32]{0:T(512)(128)(4,1)} %get-tuple-element.130) | copy-start | bytes 100
  208.9 9.3 %copy-start.48 = (f32[32]{0:T(128)S(1)}, f32[32]{0:T(128)}, u32[]{:S(2)}) copy-start(f32[32]{0:T(128)} %get-tuple-element.127) | copy-start | bytes 388
  224.2 5.0 copy-start.64
  226.2 5.2 %collective-permute-start.2 = (f32[32,2,2,128]{3,2,1,0:T(2,128)S(1)}, f32[32,2,2,128]{3,2,1,0:T(2,128)S(1)}, u32[]{:S(2)}, u32[]{:S(2)}) collective-permute-start(f32[32,2,2,128]{3,2,1,0:T(2,128)S(1)} %get-tuple-element.79), channel_id=1, source_target_pairs={{0,8},{8,16},{16,24},{24,0},{1,9},{9,17},{17,25},{25,1},{2,10},{10... | collective-permute-start | bytes 196616 | tf_op jit(solution)/shard_map/ppermute | solution.py:20
  227.3 5.3 %collective-permute-start.3 = (f32[32,2,2,128]{3,2,1,0:T(2,128)S(1)}, f32[32,2,2,128]{3,2,1,0:T(2,128)S(1)}, u32[]{:S(2)}, u32[]{:S(2)}) collective-permute-start(f32[32,2,2,128]{3,2,1,0:T(2,128)S(1)} %get-tuple-element.80), channel_id=1, source_target_pairs={{8,0},{16,8},{24,16},{0,24},{9,1},{17,9},{25,17},{1,25},{10,2},{18... | collective-permute-start | bytes 196616 | tf_op jit(solution)/shard_map/ppermute | solution.py:22
  257.9 5.6 %copy-start.44 = (pred[80]{0:T(512)(128)(4,1)S(1)}, pred[80]{0:T(512)(128)(4,1)}, u32[]{:S(2)}) copy-start(pred[80]{0:T(512)(128)(4,1)} %get-tuple-element.31) | copy-start | bytes 244
  257.9 5.6 %copy-start.45 = (pred[80]{0:T(512)(128)(4,1)S(1)}, pred[80]{0:T(512)(128)(4,1)}, u32[]{:S(2)}) copy-start(pred[80]{0:T(512)(128)(4,1)} %get-tuple-element.178) | copy-start | bytes 244
  257.9 5.6 %copy-start.46 = (pred[80]{0:T(512)(128)(4,1)S(1)}, pred[80]{0:T(512)(128)(4,1)}, u32[]{:S(2)}) copy-start(pred[80]{0:T(512)(128)(4,1)} %get-tuple-element.180) | copy-start | bytes 244
  257.9 5.6 %copy-start.53 = (pred[80]{0:T(512)(128)(4,1)S(1)}, pred[80]{0:T(512)(128)(4,1)}, u32[]{:S(2)}) copy-start(pred[80]{0:T(512)(128)(4,1)} %get-tuple-element.29) | copy-start | bytes 244
  257.9 5.6 %copy-start.60 = (f32[80]{0:T(128)S(1)}, f32[80]{0:T(128)}, u32[]{:S(2)}) copy-start(f32[80]{0:T(128)} %get-tuple-element.144) | copy-start | bytes 964
  257.9 5.6 %copy-start.61 = (f32[80]{0:T(128)S(1)}, f32[80]{0:T(128)}, u32[]{:S(2)}) copy-start(f32[80]{0:T(128)} %get-tuple-element.145) | copy-start | bytes 964
  257.9 5.6 %copy-start.62 = (f32[80]{0:T(128)S(1)}, f32[80]{0:T(128)}, u32[]{:S(2)}) copy-start(f32[80]{0:T(128)} %get-tuple-element.146) | copy-start | bytes 964
  257.9 5.6 %copy-start.63 = (f32[80]{0:T(128)S(1)}, f32[80]{0:T(128)}, u32[]{:S(2)}) copy-start(f32[80]{0:T(128)} %get-tuple-element.147) | copy-start | bytes 964
  291.0 12.4 %copy-start.55 = (pred[8]{0:T(512)(128)(4,1)S(1)}, pred[8]{0:T(512)(128)(4,1)}, u32[]{:S(2)}) copy-start(pred[8]{0:T(512)(128)(4,1)} %get-tuple-element.210) | copy-start | bytes 28
  293.5 11.5 %copy-start.54 = (pred[8]{0:T(512)(128)(4,1)S(1)}, pred[8]{0:T(512)(128)(4,1)}, u32[]{:S(2)}) copy-start(pred[8]{0:T(512)(128)(4,1)} %get-tuple-element.211) | copy-start | bytes 28
  296.1 10.4 %copy-start.59 = (pred[8]{0:T(512)(128)(4,1)S(1)}, pred[8]{0:T(512)(128)(4,1)}, u32[]{:S(2)}) copy-start(pred[8]{0:T(512)(128)(4,1)} %get-tuple-element.212) | copy-start | bytes 28
  298.6 9.4 %copy-start.58 = (pred[8]{0:T(512)(128)(4,1)S(1)}, pred[8]{0:T(512)(128)(4,1)}, u32[]{:S(2)}) copy-start(pred[8]{0:T(512)(128)(4,1)} %get-tuple-element.213) | copy-start | bytes 28
  300.9 7.3 %copy-start.57 = (pred[8]{0:T(512)(128)(4,1)S(1)}, pred[8]{0:T(512)(128)(4,1)}, u32[]{:S(2)}) copy-start(pred[8]{0:T(512)(128)(4,1)} %get-tuple-element.214) | copy-start | bytes 28
  303.4 5.1 copy-start.14
  303.4 5.1 copy-start.56
  452.8 55.8 %copy-start.1 = (f32[128,160]{0,1:T(8,128)S(1)}, f32[128,160]{0,1:T(8,128)}, u32[]{:S(2)}) copy-start(f32[128,160]{0,1:T(8,128)} %param.24) | copy-start | bytes 245764
  (42 other events, 86.4 us)
Sparse Core Ops, SparseCore 0:
  312.9 67.8 all-gather.1
where the time goes:
time: 521 us; the launch traced here: 516 us
  local copies, waits for them, and re-layouts  293 us (56%)
  other arithmetic  179 us (34%)
  matrix products  18.2 us (3%)
  between operations  15.1 us (3%)
  starting transfers between devices  7.05 us (1%)
    gather x16, local copies, waits for them, and re-layouts, aggregate(): picked = jnp.take(flat, jnp.clip(child_ids, 0, box_count - 1), axis=0)  71.2 us
    gather x1, local copies, waits for them, and re-layouts, translate(): jnp.take(operators, vectors.reshape(-1), axis=0).reshape(rows.shape)  55.5 us
    reduce_sum x1, other arithmetic, translate(): jnp.sum(picked[:, :, 0] * rows[:, :, 0] - picked[:, :, 1] * rows[:, :, 1]...  54.2 us
    gather x8, local copies, waits for them, and re-layouts, interpolate(): jnp.take(grid, local_start + offset, axis=2)  51.5 us
    gather x1, local copies, waits for them, and re-layouts, per_device(): picked = jnp.take(portion, jnp.clip(flat_src, 0, length - 1), axis=0)  45.8 us
    add x2, other arithmetic, interpolate(): summed + phi_weight[offset][None, None, :, None] * jnp.take(grid, local_s...  36.3 us
    unnamed x155, local copies, waits for them, and re-layouts  25.3 us
    reshape x3, local copies, waits for them, and re-layouts, aggregate(): flat = level.reshape(box_count, 2, level.shape[2] * level.shape[3])  25.1 us
  transfers between devices with their start and end apart: 5, of which 2 were waited for; matrix products, arithmetic and copies ran while one was open for 18% of the time, Pallas kernels for 0%

commit v1 on v0

v1 whole, which is shorter than its diff:
```python
import functools
import math

import jax
import jax.numpy as jnp
import numpy as np
from jax import lax
from jax.experimental import pallas as pl
from jax.experimental.pallas import tpu as pltpu
from jax.sharding import PartitionSpec as P

SIZE_B = 8
SIZE_C = 16
LANES = 128
GROUP = 4


def window(first, last, n_child, n_parent):
    low = 0
    while (low - 1) * n_child // n_parent + 2 >= first:
        low -= 1
    high = 0
    while (high + 1) * n_child // n_parent - 2 <= last:
        high += 1
    return low, high + 1


def phase_table(parts, per_part, low, high, n_theta, size):
    n_phi = parts * per_part
    theta = np.pi * (np.arange(n_theta) + 0.5) / n_theta
    first = np.arange(parts)[:, None] * per_part
    phi = 2.0 * np.pi * (first + np.arange(low, high)[None]) / n_phi
    u_x = np.cos(phi)[..., None] * np.sin(theta)
    u_y = np.sin(phi)[..., None] * np.sin(theta)
    u_z = np.broadcast_to(np.cos(theta), u_x.shape)
    psi = []
    for o in range(8):
        s_x, s_y, s_z = 2 * (o >> 2 & 1) - 1, 2 * (o >> 1 & 1) - 1, 2 * (o & 1) - 1
        psi.append(0.5 * np.pi * size * (s_x * u_x + s_y * u_y + s_z * u_z))
    psi = np.stack(psi, axis=2)
    return np.concatenate([np.cos(psi), np.sin(psi)], axis=2).astype(np.float32)


def split(x):
    high = x.astype(jnp.bfloat16)
    return high, (x - high.astype(jnp.float32)).astype(jnp.bfloat16)


def split_outside(x):
    high = lax.reduce_precision(x, exponent_bits=8, mantissa_bits=7)
    return high.astype(jnp.bfloat16), (x - high).astype(jnp.bfloat16)


def mm(a, b):
    return jnp.dot(a, b, preferred_element_type=jnp.float32)


def aggregate_kernel(
    steps, az_step, wb, wc, out_rows,
    samp, idx_b, wgt_b, idx_c, wgt_c,
    x_ref, tab_ref, sb_ref, phb_ref, tbc_ref, sc_ref, phc_ref,
    o_ref, grid_a, grid_b,
):
    step = pl.program_id(0)
    count_a = x_ref.shape[0]
    rows_x = x_ref.shape[1]
    rows = x_ref.reshape(count_a * rows_x, LANES)
    for c in range(2):
        for q in range(az_step // GROUP):
            tiles = [
                split(rows[pl.ds(6 * q + 2 * j + c, count_a, stride=rows_x), :]) for j in range(3)
            ]
            for pair in range(2):
                high = jnp.concatenate([tiles[pair][0], tiles[pair + 1][0]], axis=1)
                low = jnp.concatenate([tiles[pair][1], tiles[pair + 1][1]], axis=1)
                both = mm(high, tab_ref[pair, 0]) + mm(low, tab_ref[pair, 0]) + mm(high, tab_ref[pair, 1])
                for k in range(2):
                    place = step * az_step + q * GROUP + pair * 2 + k
                    grid_a[place, c * count_a : (c + 1) * count_a, :] = both[:, k * LANES : (k + 1) * LANES]

    @pl.when(step == steps - 1)
    def _():
        count_b = sb_ref.shape[0] // 8
        n_theta_c = tbc_ref.shape[2]

        def level_b(m, carry):
            parts = []
            for c in range(2):
                here = slice(c * count_a, (c + 1) * count_a)
                value = wgt_b[0, m] * grid_a[idx_b[0, m], here, :]
                for k in range(1, 4):
                    value = value + wgt_b[k, m] * grid_a[idx_b[k, m], here, :]
                parts.append(split(value))
            stacked = jnp.concatenate(
                [
                    jnp.concatenate([parts[0][0], parts[1][0]], axis=1),
                    jnp.concatenate([parts[0][1], parts[1][1]], axis=1),
                ],
                axis=0,
            )
            picked = mm(sb_ref[...], stacked)
            real = jnp.zeros((count_b, LANES), jnp.float32)
            imag = jnp.zeros((count_b, LANES), jnp.float32)
            for o in range(8):
                cosine = phb_ref[m, o : o + 1, :]
                sine = phb_ref[m, 8 + o : 9 + o, :]
                pr = picked[o * count_b : (o + 1) * count_b, :LANES]
                pi = picked[o * count_b : (o + 1) * count_b, LANES:]
                real = real + pr * cosine - pi * sine
                imag = imag + pr * sine + pi * cosine
            high, low = split(jnp.concatenate([real, imag], axis=0))
            both = jnp.concatenate([high, low], axis=1)
            grid_b[m] = mm(both, tbc_ref[0]) + mm(high, tbc_ref[1, :LANES])
            return carry

        lax.fori_loop(0, wb, level_b, 0)

        count_c = sc_ref.shape[0] // 8

        def level_c(g, carry):
            reals, imags = [], []
            for i in range(GROUP):
                n = g * GROUP + i
                value = wgt_c[0, n] * grid_b[idx_c[0, n]]
                for k in range(1, 4):
                    value = value + wgt_c[k, n] * grid_b[idx_c[k, n]]
                high, low = split(value)
                rr = mm(sc_ref[...], jnp.concatenate([high[:count_b], low[:count_b]], axis=0))
                ri = mm(sc_ref[...], jnp.concatenate([high[count_b:], low[count_b:]], axis=0))
                real = jnp.zeros((count_c, n_theta_c), jnp.float32)
                imag = jnp.zeros((count_c, n_theta_c), jnp.float32)
                for o in range(8):
                    cosine = phc_ref[n, o : o + 1, :]
                    sine = phc_ref[n, 8 + o : 9 + o, :]
                    pr = rr[o * count_c : (o + 1) * count_c]
                    pi = ri[o * count_c : (o + 1) * count_c]
                    real = real + pr * cosine - pi * sine
                    imag = imag + pr * sine + pi * cosine
                reals.append(real)
                imags.append(imag)
            for c, flat in enumerate((jnp.concatenate(reals, axis=1), jnp.concatenate(imags, axis=1))):
                tiles = flat.shape[1] // LANES
                for t in range(tiles):
                    o_ref[pl.ds(g * 2 * tiles + 2 * t + c, count_c, stride=out_rows), :] = flat[
                        :, t * LANES : (t + 1) * LANES
                    ]
            return carry

        lax.fori_loop(0, wc // GROUP, level_c, 0)


def translate_kernel(list_len, chunk, src, vec, x_ref, t_hbm, o_ref, real, imag, buf, sem):
    p = pl.program_id(0)
    count = pl.num_programs(0)
    n_src, samples = x_ref.shape[0], x_ref.shape[2]
    slot = lax.rem(p, 2)

    def fetch(target, where):
        def one(l, carry):
            pltpu.make_async_copy(
                t_hbm.at[vec[target * list_len + l]], buf.at[where, l], sem.at[where]
            ).start()
            return carry

        lax.fori_loop(0, list_len, one, 0)

    @pl.when(p == 0)
    def _():
        fetch(0, 0)

    @pl.when(p + 1 < count)
    def _():
        fetch(p + 1, 1 - slot)

    @pl.when(p == 0)
    def _():
        def one(s, carry):
            for r in range(0, samples, chunk):
                here = slice(r, r + chunk)
                real[s, :, here] = jnp.broadcast_to(x_ref[s, 0:1, here], (2, chunk))
                imag[s, :, here] = jnp.broadcast_to(x_ref[s, 1:2, here], (2, chunk))
            return carry

        lax.fori_loop(0, n_src, one, 0)

    def drain(l, carry):
        pltpu.make_async_copy(t_hbm.at[0], buf.at[slot, l], sem.at[slot]).wait()
        return carry

    lax.fori_loop(0, list_len, drain, 0)

    def one_chunk(i, carry):
        r = pl.ds(pl.multiple_of(i * chunk, chunk), chunk)
        by_real = jnp.zeros((2, chunk), jnp.float32)
        by_imag = jnp.zeros((2, chunk), jnp.float32)
        for l in range(list_len):
            s = src[p * list_len + l]
            t = buf[slot, l, :, r]
            by_real = by_real + t * real[s, :, r]
            by_imag = by_imag + t * imag[s, :, r]
        o_ref[0, 0:1, r] = by_real[0:1] - by_imag[1:2]
        o_ref[0, 1:2, r] = by_imag[0:1] + by_real[1:2]
        return carry

    lax.fori_loop(0, samples // chunk, one_chunk, 0)


def pick_chunk(samples):
    for tiles in (20, 16, 12, 8, 4, 2, 1):
        if samples % (tiles * LANES) == 0:
            return tiles * LANES
    return samples


def interleave(x):
    return x.reshape(x.shape[0], 2, -1, LANES).transpose(0, 2, 1, 3).reshape(x.shape[0], -1, LANES)


def stencil(start, weight, first, low, high, src_low, src_high, n_child):
    nearest = start - first
    tap = nearest[None, :] + jnp.arange(4, dtype=jnp.int32)[:, None]
    half = n_child // 2
    tap = (tap + half) % n_child - half
    centre = (src_low + src_high) // 2
    tap = jnp.where(tap - centre > half, tap - n_child, tap)
    tap = jnp.where(tap - centre < -half, tap + n_child, tap)
    inside = (tap >= src_low) & (tap < src_high)
    rows = jnp.clip(tap - src_low, 0, src_high - src_low - 1)
    return rows.astype(jnp.int32), jnp.where(inside, weight, 0.0)


def one_hot(children, first, count):
    ids = (children - first).T.reshape(-1)
    hot = ((ids[:, None] == jnp.arange(count)[None, :]) & (children.T.reshape(-1) >= 0)[:, None]).astype(jnp.bfloat16)
    return jnp.concatenate([hot, hot], axis=1)


def per_device(
    n_samp,
    pattern_a, children_b, children_c, theta_ab, theta_bc,
    phi_start_b, phi_weight_b, phi_start_c, phi_weight_c,
    translation, list_src, list_vec,
):
    samp = lax.axis_index("samp")
    box = lax.axis_index("box")
    count_a, count_b, count_c = pattern_a.shape[0], children_b.shape[0], children_c.shape[0]
    theta_a, theta_b = theta_ab.shape
    theta_c = theta_bc.shape[1]
    pa = pattern_a.shape[2] // theta_a
    pb = phi_start_b.shape[0]
    pc = phi_start_c.shape[0]
    n_a, n_b, n_c = n_samp * pa, n_samp * pb, n_samp * pc
    low_b, high_b = window(0, pa - 1, n_a, n_b)
    low_c, high_c = window(low_b, high_b - 1, n_b, n_c)
    ext = -(-max(-low_c, high_c - pc) // GROUP) * GROUP
    low_c, high_c = -ext, pc + ext
    wb, wc = high_b - low_b, high_c - low_c

    up = [(i, (i + 1) % n_samp) for i in range(n_samp)]
    down = [((i + 1) % n_samp, i) for i in range(n_samp)]
    table_b = jnp.concatenate([phi_start_b.astype(jnp.float32)[None], phi_weight_b], axis=0)
    table_c = jnp.concatenate([phi_start_c.astype(jnp.float32)[None], phi_weight_c], axis=0)
    near = max(ext, -low_b, high_b - pb)
    left = lax.ppermute(jnp.concatenate([table_b[:, pb - near :], table_c[:, pc - near :]], 1), "samp", up)
    right = lax.ppermute(jnp.concatenate([table_b[:, :near], table_c[:, :near]], 1), "samp", down)
    table_b = jnp.concatenate([left[:, near + low_b : near], table_b, right[:, : high_b - pb]], 1)
    table_c = jnp.concatenate([left[:, 2 * near - ext :], table_c, right[:, near : near + ext]], 1)
    idx_b, wgt_b = stencil(
        table_b[0].astype(jnp.int32), table_b[1:], samp * pa, low_b, high_b, 0, pa, n_a
    )
    idx_c, wgt_c = stencil(
        table_c[0].astype(jnp.int32), table_c[1:], samp * pb, low_c, high_c, low_b, high_b, n_b
    )

    tab = []
    for pair in range(2):
        at = pair * (2 * theta_a - LANES)
        blocks = jnp.zeros((2 * LANES, 2 * theta_b), jnp.float32)
        for k in range(2):
            blocks = lax.dynamic_update_slice(blocks, theta_ab, (at + k * theta_a, k * theta_b))
        tab.append(jnp.stack(split_outside(blocks)))
    tab = jnp.stack(tab)
    high, low = split_outside(theta_bc)
    tbc = jnp.stack([jnp.concatenate([high, high], 0), jnp.concatenate([low, low], 0)])
    s_b = one_hot(children_b, box * count_a, count_a)
    s_c = one_hot(children_c, box * count_b, count_b)
    phb = jnp.asarray(phase_table(n_samp, pb, low_b, high_b, theta_b, SIZE_B))
    phc = jnp.asarray(phase_table(n_samp, pc, low_c, high_c, theta_c, SIZE_C))

    x = interleave(pattern_a)
    steps = pa // 16 if pa % 16 == 0 else 1
    x = jnp.pad(x, ((0, 0), (0, -x.shape[1] % 8), (0, 0)))
    rows_x = x.shape[1]
    az_step = pa // steps
    tiles = GROUP * theta_c // LANES
    out_rows = wc // GROUP * 2 * tiles
    ext_rows = ext // GROUP * 2 * tiles
    rows = pc // GROUP * 2 * tiles
    one = pl.Buffered(1)
    wide = pl.pallas_call(
        functools.partial(aggregate_kernel, steps, az_step, wb, wc, out_rows),
        grid_spec=pltpu.PrefetchScalarGridSpec(
            num_scalar_prefetch=5,
            grid=(steps,),
            in_specs=[
                pl.BlockSpec((count_a, rows_x // steps, LANES), lambda i, *_: (0, i, 0)),
                pl.BlockSpec(tab.shape, lambda i, *_: (0, 0, 0, 0), pipeline_mode=one),
                pl.BlockSpec(s_b.shape, lambda i, *_: (0, 0), pipeline_mode=one),
                pl.BlockSpec((None,) + phb.shape[1:], lambda i, s, *_: (s[0], 0, 0, 0), pipeline_mode=one),
                pl.BlockSpec(tbc.shape, lambda i, *_: (0, 0, 0), pipeline_mode=one),
                pl.BlockSpec(s_c.shape, lambda i, *_: (0, 0), pipeline_mode=one),
                pl.BlockSpec((None,) + phc.shape[1:], lambda i, s, *_: (s[0], 0, 0, 0), pipeline_mode=one),
            ],
            out_specs=pl.BlockSpec((count_c * out_rows, LANES), lambda i, *_: (0, 0)),
            scratch_shapes=[
                pltpu.VMEM((pa, 2 * count_a, LANES), jnp.float32),
                pltpu.VMEM((wb, 2 * count_b, theta_c), jnp.float32),
            ],
        ),
        out_shape=jax.ShapeDtypeStruct((count_c * out_rows, LANES), jnp.float32),
        compiler_params=pltpu.CompilerParams(vmem_limit_bytes=48 << 20),
        name="aggregate",
    )(samp.reshape(1), idx_b, wgt_b, idx_c, wgt_c, x, tab, s_b, phb, tbc, s_c, phc)
    wide = wide.reshape(count_c, out_rows, LANES)
    from_left = lax.ppermute(wide[:, out_rows - ext_rows :], "samp", up)
    from_right = lax.ppermute(wide[:, :ext_rows], "samp", down)
    zeros = jnp.zeros((count_c, rows - ext_rows, LANES), jnp.float32)
    mine = (
        wide[:, ext_rows : out_rows - ext_rows]
        + jnp.concatenate([from_left, zeros], 1)
        + jnp.concatenate([zeros, from_right], 1)
    )
    mine = mine.reshape(count_c, rows // 2, 2, LANES).transpose(0, 2, 1, 3).reshape(count_c, 2, -1)
    everyone = lax.all_gather(mine, "box", axis=0, tiled=True)

    list_len = list_src.shape[1]
    n_src, _, samples = everyone.shape
    chunk = pick_chunk(samples)
    return pl.pallas_call(
        functools.partial(translate_kernel, list_len, chunk),
        grid_spec=pltpu.PrefetchScalarGridSpec(
            num_scalar_prefetch=2,
            grid=(count_c,),
            in_specs=[
                pl.BlockSpec(everyone.shape, lambda i, *_: (0, 0, 0), pipeline_mode=one),
                pl.BlockSpec(memory_space=pl.ANY),
            ],
            out_specs=pl.BlockSpec((1, 2, samples), lambda i, *_: (i, 0, 0)),
            scratch_shapes=[
                pltpu.VMEM(everyone.shape, jnp.float32),
                pltpu.VMEM(everyone.shape, jnp.float32),
                pltpu.VMEM((2, list_len, 2, samples), jnp.float32),
                pltpu.SemaphoreType.DMA((2,)),
            ],
        ),
        out_shape=jax.ShapeDtypeStruct((count_c, 2, samples), jnp.float32),
        compiler_params=pltpu.CompilerParams(vmem_limit_bytes=48 << 20),
        name="translate",
    )(list_src.reshape(-1), list_vec.reshape(-1), everyone, translation)


def solution(mesh):
    placed = (
        P("box", None, "samp"),
        P("box", None),
        P("box", None),
        P(),
        P(),
        P("samp"),
        P(None, "samp"),
        P("samp"),
        P(None, "samp"),
        P(None, None, "samp"),
        P("box", None),
        P("box", None),
    )
    return jax.shard_map(
        functools.partial(per_device, mesh.shape["samp"]),
        mesh=mesh, in_specs=placed, out_specs=P("box", None, "samp"), check_vma=False,
    )
```

time: 521 us -> 183 us (0.35)
  local copies, waits for them, and re-layouts: 293 us -> 21.9 us
  other arithmetic: 179 us -> 7.52 us
  waiting for transfers between devices: 3.42 us -> 71.5 us
  Pallas kernels: 0 us -> 59.9 us
  matrix products: 18.2 us -> 0 us
    gather x26 -> x0, local copies, waits for them, and re-layouts: 224 us -> none  [the longest x16 71.2 us: aggregate(): picked = jnp.take(flat, jnp.clip(child_ids, 0, box_count - 1), axis=0)]
    all_gather x1, waiting for transfers between devices: 0.01 us -> 66.2 us  [per_device(): everyone = lax.all_gather(mine, 'box', axis=0, tiled=True)]
    pallas_call x0 -> x2, Pallas kernels: none -> 59.9 us  [the longest x1 41.4 us: per_device(): pl.pallas_call(functools.partial(aggregate_kernel, steps, az_step, wb, wc...]
    reduce_sum x1 -> x0, other arithmetic: 54.2 us -> none  [translate(): jnp.sum(picked[:, :, 0] * rows[:, :, 0] - picked[:, :, 1] * rows[:, :, 1]...]
    select_n x25 -> x2, other arithmetic: 40.2 us -> 0.04 us  [stencil(): return (rows.astype(jnp.int32), jnp.where(inside, weight, 0.0))]
    add x4 -> x3, other arithmetic: 38.6 us -> 0.18 us  [the longest x1 0.16 us: per_device(): wide[:, ext_rows:out_rows - ext_rows]]
    reshape x4, local copies, waits for them, and re-layouts: 25.1 us -> 1.79 us  [the longest x2 1.63 us: per_device(): mine.reshape(count_c, rows // 2, 2, LANES).transpose(0, 2, 1, 3)]
    mul x12 -> x0, other arithmetic: 21.2 us -> none  [the longest x1 19.8 us: per_device(): gathered = inside * picked]
  transfers between devices with their start and end apart: 5 -> 5, of which waited for: 2 -> 3; matrix products, arithmetic and copies ran while one was open for 18% -> 13% of each run, Pallas kernels for 0% -> 0%
where the time goes in v1:
time: 183 us; the launch traced here: 181 us
  waiting for transfers between devices  71.5 us (39%)
  Pallas kernels  59.9 us (33%)
  local copies, waits for them, and re-layouts  21.9 us (12%)
  between operations  13.6 us (7%)
  other arithmetic  7.52 us (4%)
  starting transfers between devices  6.96 us (4%)
    all_gather x1, waiting for transfers between devices, per_device(): everyone = lax.all_gather(mine, 'box', axis=0, tiled=True)  66.2 us
    pallas_call x1, Pallas kernels, per_device(): pl.pallas_call(functools.partial(aggregate_kernel, steps, az_step, wb, wc...  41.4 us
    pallas_call x1, Pallas kernels, per_device(): pl.pallas_call(functools.partial(translate_kernel, list_len, chunk), grid...  18.5 us
    unnamed x14, local copies, waits for them, and re-layouts  9.14 us
    transpose x1, local copies, waits for them, and re-layouts, interleave(): x.reshape(x.shape[0], 2, -1, LANES).transpose(0, 2, 1, 3)  8.32 us
    ppermute x1, starting transfers between devices, per_device(): lax.ppermute(jnp.concatenate([table_b[:, :near], table_c[:, :near]], 1),...  3.92 us
  transfers between devices with their start and end apart: 5, of which 3 were waited for; matrix products, arithmetic and copies ran while one was open for 13% of the time, Pallas kernels for 0%

profile of v1, /device:TPU:0, one launch (start us, length us, event | category | flops | bytes accessed | tf_op | source)
XLA Modules:
  0.0 181.4 jit_solution(2948791527177083091)
XLA Ops:
  6.5 0.7 convert_bitcast_fusion.1
  7.2 0.7 convert_bitcast_fusion
  7.9 0.7 pad_maximum_fusion.2
  8.5 0.7 pad_maximum_fusion.3
  9.4 3.9 %collective-permute-start.1 = (f32[5,16]{1,0:T(8,128)S(1)}, f32[5,16]{1,0:T(8,128)S(1)}, u32[]{:S(2)}, u32[]{:S(2)}) collective-permute-start(f32[5,16]{1,0:T(8,128)S(1)} %pad_maximum_fusion.5), channel_id=1, source_target_pairs={{8,0},{16,8},{24,16},{0,24},{9,1},{17,9},{25,17},{1,25},{10,2},{18... | collective-permute-start | bytes 968 | tf_op jit(solution)/shard_map/ppermute | solution.py:265
  13.4 0.9 reduce_precision.11
  14.3 1.0 copy.45
  15.3 0.9 fusion.15
  16.2 0.7 compare_bitcast_fusion.1
  16.9 0.7 subtract_bitcast_fusion.1
  17.6 0.1 eq.34
  17.6 0.1 ge.44
  17.7 0.1 fusion.7
  17.9 0.1 copy.44
  18.0 0.7 compare_bitcast_fusion
  18.7 0.7 subtract_bitcast_fusion
  19.5 0.1 eq.38
  19.5 0.1 copy.48
  19.6 0.1 ge.48
  19.7 0.1 fusion.8
  19.9 0.8 constant_dynamic-update-slice_fusion.1
  21.0 8.1 %copy.42 = f32[128,2,4608]{0,2,1:T(8,128)} copy(f32[128,2,4608]{2,1,0:T(2,128)} %param.14) | data formatting | bytes 9437184 | tf_op args[0]
  29.1 8.3 %copy.43 = f32[128,36,2,128]{3,2,1,0:T(2,128)} copy(f32[128,36,2,128]{0,3,1,2:T(8,128)} %bitcast.45) | data formatting | bytes 9437184 | tf_op jit(solution)/shard_map/transpose | solution.py:216
  38.0 41.4 %aggregate.1 = f32[1920,128]{1,0:T(8,128)S(1)} custom-call(s32[1]{0:T(128)} %bitcast.samp, s32[4,69]{1,0:T(4,128)S(1)} %broadcast_clamp_fusion.idx_b, f32[4,69]{1,0:T(4,128)S(1)} %slice_select_fusion.1.wgt_b, s32[4,96]{1,0:T(4,128)S(1)} %add_clamp_fusion.idx_c, f32[4,96]{1,0:T(4,128)S(1)} %slice_select_fusion.wgt_c, f32[128,72,128]{2,1,0:T(8,128)} %bitcast.44, ...), custom_call_target="tpu_custom_call" | custom-call | tf_op jit(solution)/shard_map/aggregate/pallas_call | solution.py:300
  79.5 3.0 %collective-permute-start.3 = (f32[8,20,128]{2,0,1:T(8,128)S(1)}, f32[8,20,128]{2,0,1:T(8,128)S(1)}, u32[]{:S(2)}, u32[]{:S(2)}) collective-permute-start(f32[8,20,128]{2,0,1:T(8,128)S(1)} %copy.58), channel_id=1, source_target_pairs={{8,0},{16,8},{24,16},{0,24},{9,1},{17,9},{25,17},{1,25},{10,2},{18... | collective-permute-start | bytes 245768 | tf_op jit(solution)/shard_map/ppermute | solution.py:326
  82.6 1.9 %collective-permute-done.3 = f32[8,20,128]{2,0,1:T(8,128)S(1)} collective-permute-done((f32[8,20,128]{2,0,1:T(8,128)S(1)}, f32[8,20,128]{2,0,1:T(8,128)S(1)}, u32[]{:S(2)}, u32[]{:S(2)}) %collective-permute-start.3) | collective-permute-done | bytes 81952 | tf_op jit(solution)/shard_map/ppermute | solution.py:326
  84.5 3.4 %collective-permute-done.2 = f32[8,20,128]{2,0,1:T(8,128)S(1)} collective-permute-done((f32[8,20,128]{2,0,1:T(8,128)S(1)}, f32[8,20,128]{2,0,1:T(8,128)S(1)}, u32[]{:S(2)}, u32[]{:S(2)}) %collective-permute-start.2) | collective-permute-done | bytes 81952 | tf_op jit(solution)/shard_map/ppermute | solution.py:325
  87.9 0.2 fusion
  88.0 0.3 copy.54
  88.3 1.4 reshape.50
  89.9 66.2 %all-gather.2.cloned.1.call-done.x_ref = f32[64,2,12800]{2,1,0:T(2,128)} async-done(((f32[8,2,12800]{2,1,0:T(2,128)}), f32[64,2,12800]{2,1,0:T(2,128)}) %all-gather.2.cloned.1.call-update) | async-done | bytes 6553616 | tf_op jit(solution)/shard_map/all_gather | solution.py:334
  156.1 18.5 %translate.1 = f32[8,2,12800]{2,1,0:T(2,128)} custom-call(s32[256]{0:T(256)S(1)} %reshape.42.src, s32[256]{0:T(256)S(1)} %reshape.43.vec, f32[64,2,12800]{2,1,0:T(2,128)} %all-gather.2.cloned.1.call-done.x_ref, f32[316,2,12800]{2,1,0:T(2,128)} %t_hbm.1), custom_call_target="tpu_custom_call" | custom-call | tf_op jit(solution)/shard_map/translate/pallas_call | solution.py:339
  (46 shorter events, 1.5 us)
Async XLA Ops:
  6.5 149.5 %all-gather.2.cloned.1.call-start = ((), (), s32[]{:S(2)}) async-start(), calls=%async_computation | async-start | bytes 7372800 | tf_op jit(solution)/shard_map/all_gather | solution.py:334
  9.4 28.2 %collective-permute-start.1 = (f32[5,16]{1,0:T(8,128)S(1)}, f32[5,16]{1,0:T(8,128)S(1)}, u32[]{:S(2)}, u32[]{:S(2)}) collective-permute-start(f32[5,16]{1,0:T(8,128)S(1)} %pad_maximum_fusion.5), channel_id=1, source_target_pairs={{8,0},{16,8},{24,16},{0,24},{9,1},{17,9},{25,17},{1,25},{10,2},{18... | collective-permute-start | bytes 968 | tf_op jit(solution)/shard_map/ppermute | solution.py:265
  13.4 24.1 %collective-permute-start = (f32[5,16]{1,0:T(8,128)S(1)}, f32[5,16]{1,0:T(8,128)S(1)}, u32[]{:S(2)}, u32[]{:S(2)}) collective-permute-start(f32[5,16]{1,0:T(8,128)S(1)} %pad_maximum_fusion.4), channel_id=1, source_target_pairs={{0,8},{8,16},{16,24},{24,0},{1,9},{9,17},{17,25},{25,1},{2,10},{10... | collective-permute-start | bytes 968 | tf_op jit(solution)/shard_map/ppermute | solution.py:264
  29.1 8.4 %copy-start.1 = (f32[4,64]{1,0:T(4,128)S(1)}, f32[4,64]{1,0:T(4,128)}, u32[]{:S(2)}) copy-start(f32[4,64]{1,0:T(4,128)} %param.20) | copy-start | bytes 3076
  29.1 8.7 %copy-start.2 = (f32[4,80]{1,0:T(4,128)S(1)}, f32[4,80]{1,0:T(4,128)}, u32[]{:S(2)}) copy-start(f32[4,80]{1,0:T(4,128)} %param.22) | copy-start | bytes 3844
  29.1 8.8 %copy-start = (f32[4,69,16,128]{3,2,1,0:T(8,128)S(1)}, f32[4,69,16,128]{3,2,1,0:T(8,128)}, u32[]{:S(2)}) copy-start(f32[4,69,16,128]{3,2,1,0:T(8,128)} %constant.97.clone.phb_ref) | copy-start | bytes 6782980
  79.4 10.3 %copy-start.3 = (s32[8,32]{1,0:T(8,128)S(1)}, s32[8,32]{1,0:T(8,128)}, u32[]{:S(2)}) copy-start(s32[8,32]{1,0:T(8,128)} %param.24) | copy-start | bytes 3076
  79.4 10.4 %copy-start.4 = (s32[8,32]{1,0:T(8,128)S(1)}, s32[8,32]{1,0:T(8,128)}, u32[]{:S(2)}) copy-start(s32[8,32]{1,0:T(8,128)} %param.25) | copy-start | bytes 3076
  79.5 5.0 %collective-permute-start.3 = (f32[8,20,128]{2,0,1:T(8,128)S(1)}, f32[8,20,128]{2,0,1:T(8,128)S(1)}, u32[]{:S(2)}, u32[]{:S(2)}) collective-permute-start(f32[8,20,128]{2,0,1:T(8,128)S(1)} %copy.58), channel_id=1, source_target_pairs={{8,0},{16,8},{24,16},{0,24},{9,1},{17,9},{25,17},{1,25},{10,2},{18... | collective-permute-start | bytes 245768 | tf_op jit(solution)/shard_map/ppermute | solution.py:326
  82.5 5.4 %collective-permute-start.2 = (f32[8,20,128]{2,0,1:T(8,128)S(1)}, f32[8,20,128]{2,0,1:T(8,128)S(1)}, u32[]{:S(2)}, u32[]{:S(2)}) collective-permute-start(f32[8,20,128]{2,0,1:T(8,128)S(1)} %copy.57), channel_id=1, source_target_pairs={{0,8},{8,16},{16,24},{24,0},{1,9},{9,17},{17,25},{25,1},{2,10},{10... | collective-permute-start | bytes 245768 | tf_op jit(solution)/shard_map/ppermute | solution.py:325
Sparse Core Ops, SparseCore 0:
  89.8 66.2 all-gather.1
